TPU v7x, 512 devices: a whole 4x4x16 slice. The times are simulated.
512 devices in a mesh: rows: 64 (over x, z_lo, core), cols: 8 (over y, z_hi).
Axes of the slice: x: 4, y: 4, z: 16 (z_hi: 2, z_lo: 8; z = z_hi * 8 + z_lo), core: 2. Of those that a mesh axis runs over, the one named last changes fastest.
Arguments:
- features: bfloat16 [786432, 256], P(('rows', 'cols')), may hold values from -6 to 6
- adj_values: bfloat16 [6144, 3, 128, 128], P(('rows', 'cols')), may hold values from -0.3125 to 0.3125
- adj_offset: int32 [6144, 3], P(('rows', 'cols')), may hold values from -2 to 2, as said below
- adj_count: int32 [6144], P(('rows', 'cols')), may hold values from 1 to 3, as said below
- weight: bfloat16 [256, 256], replicated, may hold values from -0.375 to 0.375
- bias_vector: float32 [256], replicated, may hold values from -4 to 4
- cotangent: bfloat16 [786432, 256], P(('rows', 'cols')), may hold values from -6 to 6
Outputs:
- activated: bfloat16 [786432, 256], P(('rows', 'cols'))
- grad_features: bfloat16 [786432, 256], P(('rows', 'cols'))
- grad_weight: float32 [256, 256], replicated
- grad_bias: float32 [256], replicated
Inputs may be any that keep to these rules, and one draw needn't show every extreme that they name: Slot 0 of every row block has offset 0; the offsets of one row block are distinct, and for row block i every i + adj_offset[i, s] lies in 0 to 6143. Row block i uses its slots 0 to adj_count[i] - 1; the values and offsets of its other slots are ignored. In every draw all row blocks of one device, drawn from the seed, use all 3 slots.
All inputs are finite; a program needn't handle non-finite values.
Results may differ from a plain program's by a relative error of at most 0.0075.
Values may be sent and summed in bfloat16 or wider, within the bound.
A program may use at most 64 MiB of HBM per device.

v0:
```python
import math
import jax
import jax.numpy as jnp
from jax import lax
from jax.sharding import PartitionSpec as P

BAND = 2


def shifted(value, axis, steps):
    count = lax.axis_size(axis)
    pairs = [(source, (source + steps) % count) for source in range(count)]
    return lax.ppermute(value, axis, pairs)


def from_behind(value, axis, steps):
    count = lax.axis_size(axis)
    initial, last = (max(0, -steps), min(count, count - steps))
    return lax.ppermute(value, axis, [(source, source + steps) for source in range(initial, last)])


def fetch_lower(rim_piece):
    narrow_step = shifted(rim_piece, "cols", 1)
    wide_step = from_behind(narrow_step, "rows", 1)
    return jnp.where(lax.axis_index("cols") == 0, wide_step, narrow_step)


def fetch_upper(rim_piece):
    narrow_step = shifted(rim_piece, "cols", -1)
    wide_step = from_behind(narrow_step, "rows", -1)
    return jnp.where(lax.axis_index("cols") == lax.axis_size("cols") - 1, wide_step, narrow_step)


def spill_lower(rim_piece):
    narrow_step = shifted(rim_piece, "cols", 1)
    wide_step = from_behind(narrow_step, "rows", 1)
    return jnp.where(lax.axis_index("cols") == 0, wide_step, narrow_step)


def spill_upper(rim_piece):
    narrow_step = shifted(rim_piece, "cols", -1)
    wide_step = from_behind(narrow_step, "rows", -1)
    return jnp.where(lax.axis_index("cols") == lax.axis_size("cols") - 1, wide_step, narrow_step)


def on_device(features, adj_values, adj_offset, adj_count, weight, bias_vector, cotangent):
    blocks = adj_offset.shape[0]
    slot_total = adj_offset.shape[1]
    block_rows = adj_values.shape[2]
    feat_width = features.shape[1]
    band_reach = BAND
    span_blocks = blocks + 2 * band_reach
    rim_rows = band_reach * block_rows
    slot_index = lax.broadcasted_iota(jnp.int32, (blocks, slot_total), 1)
    block_index = lax.broadcasted_iota(jnp.int32, (blocks, slot_total), 0)
    active = slot_index < adj_count[:, None]
    target = block_index + band_reach + adj_offset
    from_below = fetch_lower(features[features.shape[0] - rim_rows :])
    from_above = fetch_upper(features[:rim_rows])
    extended = jnp.concatenate([from_below, features, from_above], 0)
    window = extended.reshape(span_blocks, block_rows, feat_width)
    picked = window[target]
    picked = jnp.where(active[:, :, None, None], picked, jnp.zeros_like(picked))
    summed = jnp.einsum("bsac,bscf->baf", adj_values, picked, preferred_element_type=jnp.float32)
    aggregated = summed.reshape(-1, feat_width).astype(jnp.bfloat16)
    preact = jnp.dot(aggregated, weight, preferred_element_type=jnp.float32) + bias_vector
    activated = jax.nn.silu(preact).astype(jnp.bfloat16)
    sigmoid_pre = jax.nn.sigmoid(preact)
    grad_pre = (
        cotangent.astype(jnp.float32) * sigmoid_pre * (1.0 + preact * (1.0 - sigmoid_pre))
    ).astype(jnp.bfloat16)
    partial_weight = lax.dot_general(
        aggregated, grad_pre, (((0,), (0,)), ((), ())), preferred_element_type=jnp.float32
    )
    partial_bias = jnp.sum(grad_pre.astype(jnp.float32), axis=0)
    total_weight, total_bias = lax.psum((partial_weight, partial_bias), ("rows", "cols"))
    nodes_total = features.shape[0] * lax.axis_size("rows") * lax.axis_size("cols")
    norm_scale = 1.0 / math.sqrt(nodes_total)
    grad_weight = total_weight * norm_scale
    grad_bias = total_bias * norm_scale
    upstream = lax.dot_general(
        grad_pre, weight, (((1,), (1,)), ((), ())), preferred_element_type=jnp.float32
    ).astype(jnp.bfloat16)
    slot_terms = jnp.einsum(
        "bsac,baf->bscf",
        adj_values,
        upstream.reshape(blocks, block_rows, feat_width),
        preferred_element_type=jnp.float32,
    )
    slot_terms = jnp.where(active[:, :, None, None], slot_terms, jnp.zeros_like(slot_terms))
    empty = jnp.zeros((span_blocks, block_rows, feat_width), jnp.float32)
    spread = empty.at[target.reshape(-1)].add(slot_terms.reshape(-1, block_rows, feat_width))
    lower_part = spread[:band_reach]
    middle = spread[band_reach : band_reach + blocks]
    upper_part = spread[band_reach + blocks :]
    from_above_dev = spill_upper(lower_part)
    from_below_dev = spill_lower(upper_part)
    combined = middle.at[:band_reach].add(from_below_dev)
    combined = combined.at[blocks - band_reach :].add(from_above_dev)
    grad_features = combined.reshape(-1, feat_width).astype(jnp.bfloat16)
    return (activated, grad_features, grad_weight, grad_bias)


def solution(mesh):
    return jax.shard_map(
        on_device,
        mesh=mesh,
        in_specs=(
            P(("rows", "cols"), None),
            P(("rows", "cols"), None, None, None),
            P(("rows", "cols"), None),
            P(("rows", "cols")),
            P(),
            P(),
            P(("rows", "cols"), None),
        ),
        out_specs=(P(("rows", "cols"), None), P(("rows", "cols"), None), P(), P()),
        check_vma=False,
    )
```

profile of v0, /device:TPU:4, one launch (start us, length us, event | category | flops | bytes accessed | tf_op | source)
XLA Modules:
  0.0 578.7 jit_solution(4762388384572714263)
XLA Ops:
  7.2 1.1 fusion.11
  8.4 15.7 %collective-permute-start = (bf16[256,256]{1,0:T(8,128)(2,1)S(1)}, bf16[256,256]{1,0:T(8,128)(2,1)S(1)}, u32[]{:S(2)}, u32[]{:S(2)}) collective-permute-start(bf16[256,256]{1,0:T(8,128)(2,1)S(1)} %get-tuple-element.35), channel_id=1, source_target_pairs={{0,1},{1,2},{2,3},{3,4},{4,5},{5,6},{6,7},{7,0},{8,9},{9,10},{10,1... | collective-permute-start | bytes 393224 | tf_op jit(solution)/shard_map/ppermute | solution.py:13
  24.1 4.4 collective-permute-start.2
  28.5 0.7 compare_select_fusion
  29.3 0.7 iota_compare_fusion
  30.1 0.2 collective-permute-done
  30.3 1.9 collective-permute-start.1
  32.4 19.6 %collective-permute-done.2 = bf16[256,256]{1,0:T(8,128)(2,1)S(1)} collective-permute-done((bf16[256,256]{1,0:T(8,128)(2,1)S(1)}, bf16[256,256]{1,0:T(8,128)(2,1)S(1)}, u32[]{:S(2)}, u32[]{:S(2)}) %collective-permute-start.2) | collective-permute-done | bytes 131104 | tf_op jit(solution)/shard_map/ppermute | solution.py:13
  52.0 1.9 collective-permute-start.3
  54.0 2.5 collective-permute-done.3
  56.6 2.3 gather_fusion
  58.9 2.4 bitcast_convert_fusion
  61.3 1.8 convert_reduce_fusion
  63.1 0.9 copy-done.2
  64.0 0.4 convolution_convert_fusion
  64.4 3.1 broadcast_select_fusion
  67.5 6.1 %copy.17 = f32[36,128,256]{2,1,0:T(8,128)} copy(f32[36,128,256]{1,2,0:T(8,128)} %bitcast.28) | data formatting | bytes 9437184 | tf_op jit(solution)/shard_map/reshape | solution.py:92
  73.9 8.9 %scatter_fusion = f32[16,128,256]{2,1,0:T(8,128)S(1)} fusion(f32[16,128,256]{2,1,0:T(8,128)S(1)} %broadcast_in_dim.36, s32[36]{0:T(128)S(1)} %fusion.8, f32[36,128,256]{2,1,0:T(8,128)} %copy.17), kind=kCustom, calls=%fused_computation.1 | custom fusion | flops 1179648 | bytes 14155920 | tf_op jit(solution)/shard_map/scatter-add | solution.py:92
  82.7 0.8 fusion.10
  83.6 8.7 %collective-permute-start.4 = (f32[2,128,256]{2,1,0:T(8,128)}, f32[2,128,256]{2,1,0:T(8,128)}, u32[]{:S(2)}, u32[]{:S(2)}) collective-permute-start(f32[2,128,256]{2,1,0:T(8,128)} %get-tuple-element.33), channel_id=1, source_target_pairs={{0,1},{1,2},{2,3},{3,4},{4,5},{5,6},{6,7},{7,0},{8,9},{9,10},{10,1... | collective-permute-start | bytes 786440 | tf_op jit(solution)/shard_map/ppermute | solution.py:13
  92.3 7.9 %collective-permute-start.6 = (f32[2,128,256]{2,1,0:T(8,128)}, f32[2,128,256]{2,1,0:T(8,128)S(1)}, u32[]{:S(2)}, u32[]{:S(2)}) collective-permute-start(f32[2,128,256]{2,1,0:T(8,128)} %get-tuple-element.32), channel_id=1, source_target_pairs={{0,7},{1,0},{2,1},{3,2},{4,3},{5,4},{6,5},{7,6},{8,15},{9,8},{10,9... | collective-permute-start | bytes 786440 | tf_op jit(solution)/shard_map/ppermute | solution.py:13
  100.2 2.5 fusion.12
  102.8 108.2 %psum.15 = f32[256]{0:T(256)S(1)} all-reduce(f32[256]{0:T(256)S(1)} %get-tuple-element.28), channel_id=1, replica_groups=mesh['rows'=64,'cols'=8] {'rows','cols'}, use_global_device_ids=true, to_apply=%region_3.4 | all-reduce | flops 256 | bytes 2048 | tf_op jit(solution)/shard_map/psum | solution.py:76
  210.9 1.9 collective-permute-start.5
  212.8 0.6 broadcast_multiply_fusion.1
  213.4 1.3 slice.73
  214.7 11.1 %collective-permute-start.7 = (f32[2,128,256]{2,1,0:T(8,128)S(1)}, f32[2,128,256]{2,1,0:T(8,128)}, u32[]{:S(2)}, u32[]{:S(2)}) collective-permute-start(f32[2,128,256]{2,1,0:T(8,128)S(1)} %collective-permute-done.6), channel_id=1, source_target_pairs={{8,0},{16,8},{24,16},{32,24},{40,32},{48,40},{56,48},{64,56},{72,6... | collective-permute-start | bytes 786440 | tf_op jit(solution)/shard_map/ppermute | solution.py:19
  225.9 338.5 %all-reduce.2.cloned.1.call-done = f32[256,256]{1,0:T(8,128)} async-done(((f32[256,256]{1,0:T(8,128)}), f32[256,256]{1,0:T(8,128)}) %all-reduce.2.cloned.1.call-update) | async-done | bytes 262160 | tf_op jit(solution)/shard_map/psum | solution.py:76
  564.3 1.7 broadcast_multiply_fusion
  566.0 1.7 fusion.7
  567.7 1.7 fusion.6
  569.5 2.4 convert_element_type.37
  (31 shorter events, 0.8 us)
Async XLA Ops:
  7.2 51.7 %copy-start = (bf16[12,3,128,128]{3,2,1,0:T(8,128)(2,1)S(1)}, bf16[12,3,128,128]{3,2,1,0:T(8,128)(2,1)}, u32[]{:S(2)}) copy-start(bf16[12,3,128,128]{3,2,1,0:T(8,128)(2,1)} %param.12) | copy-start | bytes 3538948
  7.2 49.3 %copy-start.1 = (bf16[1536,256]{1,0:T(8,128)(2,1)S(1)}, bf16[1536,256]{1,0:T(8,128)(2,1)}, u32[]{:S(2)}) copy-start(bf16[1536,256]{1,0:T(8,128)(2,1)} %param.11) | copy-start | bytes 2359300
  7.2 557.1 %all-reduce.2.cloned.1.call-start = ((), (), s32[]{:S(2)}) async-start(), calls=%async_computation | async-start | bytes 524288 | tf_op jit(solution)/shard_map/psum | solution.py:76
  8.4 22.0 %collective-permute-start = (bf16[256,256]{1,0:T(8,128)(2,1)S(1)}, bf16[256,256]{1,0:T(8,128)(2,1)S(1)}, u32[]{:S(2)}, u32[]{:S(2)}) collective-permute-start(bf16[256,256]{1,0:T(8,128)(2,1)S(1)} %get-tuple-element.35), channel_id=1, source_target_pairs={{0,1},{1,2},{2,3},{3,4},{4,5},{5,6},{6,7},{7,0},{8,9},{9,10},{10,1... | collective-permute-start | bytes 393224 | tf_op jit(solution)/shard_map/ppermute | solution.py:13
  24.1 28.0 %collective-permute-start.2 = (bf16[256,256]{1,0:T(8,128)(2,1)S(1)}, bf16[256,256]{1,0:T(8,128)(2,1)S(1)}, u32[]{:S(2)}, u32[]{:S(2)}) collective-permute-start(bf16[256,256]{1,0:T(8,128)(2,1)S(1)} %get-tuple-element.36), channel_id=1, source_target_pairs={{0,7},{1,0},{2,1},{3,2},{4,3},{5,4},{6,5},{7,6},{8,15},{9,8},{10,9... | collective-permute-start | bytes 393224 | tf_op jit(solution)/shard_map/ppermute | solution.py:13
  30.3 23.7 %collective-permute-start.1 = (bf16[256,256]{1,0:T(8,128)(2,1)S(1)}, bf16[256,256]{1,0:T(8,128)(2,1)S(1)}, u32[]{:S(2)}, u32[]{:S(2)}) collective-permute-start(bf16[256,256]{1,0:T(8,128)(2,1)S(1)} %collective-permute-done), channel_id=1, source_target_pairs={{0,8},{8,16},{16,24},{24,32},{32,40},{40,48},{48,56},{56,64},{64,7... | collective-permute-start | bytes 393224 | tf_op jit(solution)/shard_map/ppermute | solution.py:19
  52.0 4.4 collective-permute-start.3
  58.9 2.4 copy-start.3
  58.9 2.4 copy-start.4
  58.9 2.5 copy-start.5
  61.3 1.9 copy-start.6
  63.1 0.9 copy-start.2
  83.6 127.3 %collective-permute-start.4 = (f32[2,128,256]{2,1,0:T(8,128)}, f32[2,128,256]{2,1,0:T(8,128)}, u32[]{:S(2)}, u32[]{:S(2)}) collective-permute-start(f32[2,128,256]{2,1,0:T(8,128)} %get-tuple-element.33), channel_id=1, source_target_pairs={{0,1},{1,2},{2,3},{3,4},{4,5},{5,6},{6,7},{7,0},{8,9},{9,10},{10,1... | collective-permute-start | bytes 786440 | tf_op jit(solution)/shard_map/ppermute | solution.py:13
  92.3 122.4 %collective-permute-start.6 = (f32[2,128,256]{2,1,0:T(8,128)}, f32[2,128,256]{2,1,0:T(8,128)S(1)}, u32[]{:S(2)}, u32[]{:S(2)}) collective-permute-start(f32[2,128,256]{2,1,0:T(8,128)} %get-tuple-element.32), channel_id=1, source_target_pairs={{0,7},{1,0},{2,1},{3,2},{4,3},{5,4},{6,5},{7,6},{8,15},{9,8},{10,9... | collective-permute-start | bytes 786440 | tf_op jit(solution)/shard_map/ppermute | solution.py:13
  210.9 355.1 %collective-permute-start.5 = (f32[2,128,256]{2,1,0:T(8,128)}, f32[2,128,256]{2,1,0:T(8,128)}, u32[]{:S(2)}, u32[]{:S(2)}) collective-permute-start(f32[2,128,256]{2,1,0:T(8,128)} %collective-permute-done.4), channel_id=1, source_target_pairs={{0,8},{8,16},{16,24},{24,32},{32,40},{40,48},{48,56},{56,64},{64,7... | collective-permute-start | bytes 786440 | tf_op jit(solution)/shard_map/ppermute | solution.py:19
  214.7 353.0 %collective-permute-start.7 = (f32[2,128,256]{2,1,0:T(8,128)S(1)}, f32[2,128,256]{2,1,0:T(8,128)}, u32[]{:S(2)}, u32[]{:S(2)}) collective-permute-start(f32[2,128,256]{2,1,0:T(8,128)S(1)} %collective-permute-done.6), channel_id=1, source_target_pairs={{8,0},{16,8},{24,16},{32,24},{40,32},{48,40},{56,48},{64,56},{72,6... | collective-permute-start | bytes 786440 | tf_op jit(solution)/shard_map/ppermute | solution.py:19
Sparse Core Ops, SparseCore 0:
  102.9 461.4 all-reduce.1
where the time goes:
time: 579 us
  waiting for transfers between devices  361 us (62%)
  blocking collectives  108 us (19%)
  starting transfers between devices  53.7 us (9%)
  other arithmetic  18.4 us (3%)
  between operations  14.3 us (2%)
  local copies, waits for them, and re-layouts  13.2 us (2%)
  matrix products  10.2 us (2%)
    psum x1, waiting for transfers between devices, on_device(): lax.psum((partial_weight, partial_bias), ('rows', 'cols'))  338 us
    psum x1, blocking collectives, on_device(): lax.psum((partial_weight, partial_bias), ('rows', 'cols'))  108 us
    ppermute x4, starting transfers between devices, shifted(): return lax.ppermute(value, axis, pairs)  36.7 us
    ppermute x4, waiting for transfers between devices, shifted(): return lax.ppermute(value, axis, pairs)  19.8 us
    ppermute x4, starting transfers between devices, from_behind(): lax.ppermute(value, axis, [(source, source + steps) for source in range(i...  16.9 us
  transfers between devices with their start and end apart: 9, of which 4 were waited for; matrix products, arithmetic and copies ran while one was open for 2% of the time, Pallas kernels for 0%

commit v1 on v0

--- a/solution.py
+++ b/solution.py
@@ -3,6 +3,7 @@
 import jax.numpy as jnp
 from jax import lax
 from jax.sharding import PartitionSpec as P
+from jax.lax import psum
 
 BAND = 2
 
@@ -73,7 +74,7 @@
         aggregated, grad_pre, (((0,), (0,)), ((), ())), preferred_element_type=jnp.float32
     )
     partial_bias = jnp.sum(grad_pre.astype(jnp.float32), axis=0)
-    total_weight, total_bias = lax.psum((partial_weight, partial_bias), ("rows", "cols"))
+    total_weight, total_bias = psum(psum((partial_weight, partial_bias), "rows"), "cols")
     nodes_total = features.shape[0] * lax.axis_size("rows") * lax.axis_size("cols")
     norm_scale = 1.0 / math.sqrt(nodes_total)
     grad_weight = total_weight * norm_scale

time: 579 us -> 1060 us (1.83)
  the two profiles are of different devices: /device:TPU:4 before, /device:TPU:2 now
where the time goes in v1:
time: 1060 us
  waiting for transfers between devices  712 us (67%)
  blocking collectives  243 us (23%)
  starting transfers between devices  44.5 us (4%)
  other arithmetic  18.4 us (2%)
  between operations  14.3 us (1%)
  local copies, waits for them, and re-layouts  13.1 us (1%)
    psum x1, waiting for transfers between devices, on_device(): psum((partial_weight, partial_bias), 'rows')  478 us
    psum x1, blocking collectives, on_device(): psum((partial_weight, partial_bias), 'rows')  200 us
    psum x1, waiting for transfers between devices, on_device(): psum(psum((partial_weight, partial_bias), 'rows'), 'cols')  184 us
    ppermute x4, waiting for transfers between devices, shifted(): return lax.ppermute(value, axis, pairs)  48 us
    psum x1, blocking collectives, on_device(): psum(psum((partial_weight, partial_bias), 'rows'), 'cols')  42.3 us
    ppermute x4, starting transfers between devices, shifted(): return lax.ppermute(value, axis, pairs)  36.7 us
  transfers between devices with their start and end apart: 10, of which 6 were waited for; matrix products, arithmetic and copies ran while one was open for 1% of the time, Pallas kernels for 0%

profile of v1, /device:TPU:2, one launch (start us, length us, event | category | flops | bytes accessed | tf_op | source)
XLA Modules:
  0.0 1055.0 jit_solution(18281853844139140296)
XLA Ops:
  7.2 1.1 fusion.11
  8.4 15.7 %collective-permute-start = (bf16[256,256]{1,0:T(8,128)(2,1)S(1)}, bf16[256,256]{1,0:T(8,128)(2,1)S(1)}, u32[]{:S(2)}, u32[]{:S(2)}) collective-permute-start(bf16[256,256]{1,0:T(8,128)(2,1)S(1)} %get-tuple-element.35), channel_id=1, source_target_pairs={{0,1},{1,2},{2,3},{3,4},{4,5},{5,6},{6,7},{7,0},{8,9},{9,10},{10,1... | collective-permute-start | bytes 393224 | tf_op jit(solution)/shard_map/ppermute | solution.py:14
  24.1 4.4 collective-permute-start.2
  28.5 0.7 compare_select_fusion
  29.3 0.7 iota_compare_fusion
  30.3 1.9 collective-permute-start.1
  32.4 19.6 %collective-permute-done.2 = bf16[256,256]{1,0:T(8,128)(2,1)S(1)} collective-permute-done((bf16[256,256]{1,0:T(8,128)(2,1)S(1)}, bf16[256,256]{1,0:T(8,128)(2,1)S(1)}, u32[]{:S(2)}, u32[]{:S(2)}) %collective-permute-start.2) | collective-permute-done | bytes 131104 | tf_op jit(solution)/shard_map/ppermute | solution.py:14
  52.0 1.9 collective-permute-start.3
  54.0 2.5 collective-permute-done.3
  56.6 2.3 gather_fusion
  58.9 2.4 bitcast_convert_fusion
  61.3 1.8 convert_reduce_fusion
  63.1 0.9 copy-done.2
  64.4 3.1 broadcast_select_fusion
  67.5 6.1 copy.17
  73.8 8.8 scatter_fusion
  82.7 0.8 fusion.10
  83.5 8.7 collective-permute-start.4
  92.2 7.9 collective-permute-start.6
  100.2 2.5 fusion.12
  102.7 28.1 %collective-permute-done.4 = f32[2,128,256]{2,1,0:T(8,128)} collective-permute-done((f32[2,128,256]{2,1,0:T(8,128)}, f32[2,128,256]{2,1,0:T(8,128)}, u32[]{:S(2)}, u32[]{:S(2)}) %collective-permute-start.4) | collective-permute-done | bytes 262176 | tf_op jit(solution)/shard_map/ppermute | solution.py:14
  130.8 1.9 collective-permute-start.5
  132.8 200.3 %psum.30 = f32[256]{0:T(256)S(1)} all-reduce(f32[256]{0:T(256)S(1)} %get-tuple-element.28), channel_id=1, replica_groups=mesh['rows'=64,'cols'=8] {'rows'}, use_global_device_ids=true, to_apply=%region_4.5 | all-reduce | flops 256 | bytes 2048 | tf_op jit(solution)/shard_map/psum | solution.py:77
  333.0 42.3 %psum.31 = f32[256]{0:T(256)S(1)} all-reduce(f32[256]{0:T(256)S(1)} %psum.30), channel_id=1, replica_groups=mesh['rows'=64,'cols'=8] {'cols'}, use_global_device_ids=true, to_apply=%region_5.6 | all-reduce | flops 256 | bytes 2048 | tf_op jit(solution)/shard_map/psum | solution.py:77
  375.4 1.9 collective-permute-start.7
  377.8 1.3 slice.73
  379.2 477.6 %all-reduce.3.cloned.1.call-done = f32[256,256]{1,0:T(8,128)} async-done(((f32[256,256]{1,0:T(8,128)}), f32[256,256]{1,0:T(8,128)}) %all-reduce.3.cloned.1.call-update) | async-done | bytes 262160 | tf_op jit(solution)/shard_map/psum | solution.py:77
  856.9 1.7 fusion.7
  858.6 1.7 fusion.6
  860.3 2.4 convert_element_type.37
  862.7 183.8 %all-reduce.5.cloned.1.call-done = f32[256,256]{1,0:T(8,128)} async-done(((f32[256,256]{1,0:T(8,128)}), f32[256,256]{1,0:T(8,128)}) %all-reduce.5.cloned.1.call-update) | async-done | bytes 262160 | tf_op jit(solution)/shard_map/psum | solution.py:77
  1046.5 1.7 broadcast_multiply_fusion
  (35 shorter events, 2.0 us)
Async XLA Ops:
  7.2 51.7 %copy-start = (bf16[12,3,128,128]{3,2,1,0:T(8,128)(2,1)S(1)}, bf16[12,3,128,128]{3,2,1,0:T(8,128)(2,1)}, u32[]{:S(2)}) copy-start(bf16[12,3,128,128]{3,2,1,0:T(8,128)(2,1)} %param.12) | copy-start | bytes 3538948
  7.2 49.3 %copy-start.1 = (bf16[1536,256]{1,0:T(8,128)(2,1)S(1)}, bf16[1536,256]{1,0:T(8,128)(2,1)}, u32[]{:S(2)}) copy-start(bf16[1536,256]{1,0:T(8,128)(2,1)} %param.11) | copy-start | bytes 2359300
  7.2 849.6 %all-reduce.3.cloned.1.call-start = ((), (), s32[]{:S(2)}) async-start(), calls=%async_computation | async-start | bytes 524288 | tf_op jit(solution)/shard_map/psum | solution.py:77
  8.4 22.0 %collective-permute-start = (bf16[256,256]{1,0:T(8,128)(2,1)S(1)}, bf16[256,256]{1,0:T(8,128)(2,1)S(1)}, u32[]{:S(2)}, u32[]{:S(2)}) collective-permute-start(bf16[256,256]{1,0:T(8,128)(2,1)S(1)} %get-tuple-element.35), channel_id=1, source_target_pairs={{0,1},{1,2},{2,3},{3,4},{4,5},{5,6},{6,7},{7,0},{8,9},{9,10},{10,1... | collective-permute-start | bytes 393224 | tf_op jit(solution)/shard_map/ppermute | solution.py:14
  24.1 28.0 %collective-permute-start.2 = (bf16[256,256]{1,0:T(8,128)(2,1)S(1)}, bf16[256,256]{1,0:T(8,128)(2,1)S(1)}, u32[]{:S(2)}, u32[]{:S(2)}) collective-permute-start(bf16[256,256]{1,0:T(8,128)(2,1)S(1)} %get-tuple-element.36), channel_id=1, source_target_pairs={{0,7},{1,0},{2,1},{3,2},{4,3},{5,4},{6,5},{7,6},{8,15},{9,8},{10,9... | collective-permute-start | bytes 393224 | tf_op jit(solution)/shard_map/ppermute | solution.py:14
  30.3 23.7 %collective-permute-start.1 = (bf16[256,256]{1,0:T(8,128)(2,1)S(1)}, bf16[256,256]{1,0:T(8,128)(2,1)S(1)}, u32[]{:S(2)}, u32[]{:S(2)}) collective-permute-start(bf16[256,256]{1,0:T(8,128)(2,1)S(1)} %collective-permute-done), channel_id=1, source_target_pairs={{0,8},{8,16},{16,24},{24,32},{32,40},{40,48},{48,56},{56,64},{64,7... | collective-permute-start | bytes 393224 | tf_op jit(solution)/shard_map/ppermute | solution.py:20
  52.0 4.4 collective-permute-start.3
  58.9 2.4 copy-start.3
  58.9 2.4 copy-start.4
  58.9 2.4 copy-start.5
  61.3 1.9 copy-start.6
  63.1 0.9 copy-start.2
  83.5 47.3 %collective-permute-start.4 = (f32[2,128,256]{2,1,0:T(8,128)}, f32[2,128,256]{2,1,0:T(8,128)}, u32[]{:S(2)}, u32[]{:S(2)}) collective-permute-start(f32[2,128,256]{2,1,0:T(8,128)} %get-tuple-element.33), channel_id=1, source_target_pairs={{0,1},{1,2},{2,3},{3,4},{4,5},{5,6},{6,7},{7,0},{8,9},{9,10},{10,1... | collective-permute-start | bytes 786440 | tf_op jit(solution)/shard_map/ppermute | solution.py:14
  92.2 283.1 %collective-permute-start.6 = (f32[2,128,256]{2,1,0:T(8,128)}, f32[2,128,256]{2,1,0:T(8,128)S(1)}, u32[]{:S(2)}, u32[]{:S(2)}) collective-permute-start(f32[2,128,256]{2,1,0:T(8,128)} %get-tuple-element.32), channel_id=1, source_target_pairs={{0,7},{1,0},{2,1},{3,2},{4,3},{5,4},{6,5},{7,6},{8,15},{9,8},{10,9... | collective-permute-start | bytes 786440 | tf_op jit(solution)/shard_map/ppermute | solution.py:14
  102.7 943.8 %all-reduce.5.cloned.1.call-start = ((), (), s32[]{:S(2)}) async-start(), calls=%async_computation.1 | async-start | bytes 524288 | tf_op jit(solution)/shard_map/psum | solution.py:77
  130.8 726.0 %collective-permute-start.5 = (f32[2,128,256]{2,1,0:T(8,128)}, f32[2,128,256]{2,1,0:T(8,128)}, u32[]{:S(2)}, u32[]{:S(2)}) collective-permute-start(f32[2,128,256]{2,1,0:T(8,128)} %collective-permute-done.4), channel_id=1, source_target_pairs={{0,8},{8,16},{16,24},{24,32},{32,40},{40,48},{48,56},{56,64},{64,7... | collective-permute-start | bytes 786440 | tf_op jit(solution)/shard_map/ppermute | solution.py:20
  375.4 483.2 %collective-permute-start.7 = (f32[2,128,256]{2,1,0:T(8,128)S(1)}, f32[2,128,256]{2,1,0:T(8,128)}, u32[]{:S(2)}, u32[]{:S(2)}) collective-permute-start(f32[2,128,256]{2,1,0:T(8,128)S(1)} %collective-permute-done.6), channel_id=1, source_target_pairs={{8,0},{16,8},{24,16},{32,24},{40,32},{48,40},{56,48},{64,56},{72,6... | collective-permute-start | bytes 786440 | tf_op jit(solution)/shard_map/ppermute | solution.py:20
Sparse Core Ops, SparseCore 0:
  102.8 754.0 all-reduce.2
  860.0 186.4 all-reduce.4
